TPU v7x, 32 devices: a whole 2x2x4 slice. The times are simulated.
32 devices in a mesh: beam: 2 (over x), freq: 8 (over z, y), tm: 2 (over core).
Axes of the slice: x: 2, y: 2, z: 4, core: 2. Of those that a mesh axis runs over, the one named last changes fastest.
Arguments:
- spectra: float32 [4096, 5120], P(('beam', 'freq'), 'tm'), parts along dimension 0, may hold values from -6 to 6
- delays: int32 [11, 2048], replicated, may hold values from 0 to 1024, as said below
- widths: int32 [8], replicated, may hold values from 1 to 128, as said below
Outputs:
- filtered: float32 [8, 4096, 5120], P(None, ('beam', 'freq'), 'tm'), parts along dimension 1
There are 2 independent parts, one for each index of `beam`. A program takes and returns all parts, laid end to end along the dimension named above; an argument that names none is the same for every part. Nothing has to cross between parts.
Inputs may be any that keep to these rules, and one draw needn't show every extreme that they name: delays[l, r] lies in 0 to 2 ** l, and every level l has some entry equal to 2 ** l. The widths include 1 and 128.
All inputs are finite; a program needn't handle non-finite values.
Results may differ from a plain program's by a relative error of at most 0.0003.
Values sent between devices are 32-bit elements; how exact they have to be, the bound alone decides.
A program may use at most 192 MiB of HBM per device.

v0:
```python
import jax
import jax.numpy as jnp
from jax import lax
from jax.sharding import PartitionSpec as P

F = 2048
TAPS = 128


def passed_along(value, axis, steps):
    count = lax.axis_size(axis)
    initial, last = (max(0, -steps), min(count, count - steps))
    return lax.ppermute(value, axis, [(source, source + steps) for source in range(initial, last)])


def from_partner(value, axis, stride):
    mask = 2**stride
    pairs = [(source, source ^ mask) for source in range(lax.axis_size(axis))]
    return lax.ppermute(value, axis, pairs)


def delay_rows(source_rows, row_shifts, out_width):
    total_width = source_rows.shape[1]
    top_reach = total_width - out_width
    shift_col = row_shifts[:, None]
    low_part = shift_col % top_reach
    result = source_rows
    bit_value = 1
    while bit_value < top_reach:
        width_now = result.shape[1]
        chosen = low_part // bit_value % 2 == 1
        result = jnp.where(chosen, result[:, bit_value:], result[:, : width_now - bit_value])
        bit_value = bit_value * 2
    lower_shift = result[:, :out_width]
    top_shift = source_rows[:, top_reach : top_reach + out_width]
    return jnp.where(shift_col == top_reach, top_shift, lower_shift)


def delay_block(current, row_shifts, half_rows, out_width):
    row_count, total_width = current.shape
    group_count = row_count // (2 * half_rows)
    block_view = current.reshape(group_count, 2, half_rows, total_width)
    source_rows = jnp.broadcast_to(
        block_view[:, 1][:, None], (group_count, 2, half_rows, total_width)
    )
    delayed = delay_rows(source_rows.reshape(row_count, total_width), row_shifts, out_width)
    summed = block_view[:, 0, :, :out_width][:, None] + delayed.reshape(
        group_count, 2, half_rows, out_width
    )
    return summed.reshape(row_count, out_width)


def local(spectra, delays, widths):
    row_count, time_span = spectra.shape
    local_levels = row_count.bit_length() - 1
    freq_count = lax.axis_size("freq")
    cross_levels = freq_count.bit_length() - 1
    position = lax.axis_index("freq")

    def own_shifts(tree_level):
        return lax.dynamic_slice_in_dim(delays[tree_level], position * row_count, row_count)

    current = spectra
    rim_depth = 2**local_levels - 1
    leading = passed_along(current[:, :rim_depth], "tm", -1)
    current = jnp.concatenate([current, leading], axis=1)
    for tree_level in range(local_levels):
        current = delay_block(
            current, own_shifts(tree_level), 2**tree_level, current.shape[1] - 2**tree_level
        )
    for bit_index in range(cross_levels):
        tree_level = local_levels + bit_index
        reach = 2**tree_level
        leading = passed_along(current[:, :reach], "tm", -1)
        own_ext = jnp.concatenate([current, leading], axis=1)
        partner_ext = from_partner(own_ext, "freq", bit_index)
        is_lower = position // 2**bit_index % 2 == 0
        first_term = jnp.where(is_lower, own_ext[:, :time_span], partner_ext[:, :time_span])
        second_source = jnp.where(is_lower, partner_ext, own_ext)
        current = first_term + delay_rows(second_source, own_shifts(tree_level), time_span)
    leading = passed_along(current[:, :TAPS], "tm", -1)
    extended = jnp.concatenate([current, leading], axis=1)
    block_count = time_span // TAPS
    block_view = extended.reshape(row_count, block_count + 1, TAPS)
    paired = jnp.concatenate([block_view[:, :-1], block_view[:, 1:]], axis=2)
    filter_count = widths.shape[0]
    input_pos = lax.broadcasted_iota(jnp.int32, (2 * TAPS, filter_count, TAPS), 0)
    output_pos = lax.broadcasted_iota(jnp.int32, (2 * TAPS, filter_count, TAPS), 2)
    distance = input_pos - output_pos
    box_widths = widths[None, :, None]
    scaling = 1.0 / jnp.sqrt(widths.astype(jnp.float32) * F)
    filter_matrix = jnp.where(
        (distance >= 0) & (distance < box_widths), scaling[None, :, None], 0.0
    )
    filter_matrix = filter_matrix.reshape(2 * TAPS, filter_count * TAPS)
    product = jnp.einsum("rbj,jk->rbk", paired, filter_matrix, precision=lax.Precision.HIGHEST)
    product = product.reshape(row_count, block_count, filter_count, TAPS)
    return jnp.transpose(product, (2, 0, 1, 3)).reshape(filter_count, row_count, time_span)


def solution(mesh):
    return jax.shard_map(
        local,
        mesh=mesh,
        in_specs=(P(("beam", "freq"), "tm"), P(), P()),
        out_specs=P(None, ("beam", "freq"), "tm"),
        check_vma=False,
    )
```

profile of v0, /device:TPU:0, one launch (start us, length us, event | category | flops | bytes accessed | tf_op | source)
XLA Modules:
  0.0 525.5 jit_solution(16496791616469396781)
XLA Ops:
  6.6 3.5 pad_maximum_fusion.2
  10.1 3.5 reshape.3247
  16.1 4.8 slice_reduce_fusion
  21.0 3.1 add.1172
  26.8 3.6 broadcast_in_dim.600
  32.8 3.9 reshape.3248
  44.1 3.6 broadcast_in_dim.604
  47.8 3.6 reshape.3249
  55.0 4.6 reshape.3250
  59.7 3.7 copy_add_fusion
  70.8 3.0 reshape.3251
  73.8 3.3 add.1183
  77.1 4.6 add.1184
  120.2 5.5 %add.1228 = f32[2,128,2560]{1,0,2:T(2,128)S(1)} broadcast(f32[128,2560]{0,1:T(8,128)S(1)} %copy.31), dimensions={1,2} | broadcast | bytes 3932160 | tf_op jit(solution)/shard_map/add | solution.py:47
  132.0 3.0 collective-permute-start.2
  135.0 63.0 %collective-permute-done.2 = f32[256,2816]{0,1:T(8,128)} collective-permute-done((f32[256,2816]{0,1:T(8,128)}, f32[256,2816]{0,1:T(8,128)}, u32[]{:S(2)}, u32[]{:S(2)}) %collective-permute-start.2) | collective-permute-done | bytes 2883616 | tf_op jit(solution)/shard_map/ppermute | solution.py:19
  214.7 68.0 %collective-permute-done.4 = f32[256,3072]{0,1:T(8,128)} collective-permute-done((f32[256,3072]{0,1:T(8,128)}, f32[256,3072]{0,1:T(8,128)}, u32[]{:S(2)}, u32[]{:S(2)}) %collective-permute-start.4) | collective-permute-done | bytes 3145760 | tf_op jit(solution)/shard_map/ppermute | solution.py:19
  293.1 3.0 collective-permute-done.5
  301.1 157.7 %collective-permute-done.6 = f32[256,3584]{0,1:T(8,128)} collective-permute-done((f32[256,3584]{0,1:T(8,128)}, f32[256,3584]{0,1:T(8,128)}, u32[]{:S(2)}, u32[]{:S(2)}) %collective-permute-start.6) | collective-permute-done | bytes 3670048 | tf_op jit(solution)/shard_map/ppermute | solution.py:19
  470.8 3.0 fusion.149
  475.9 3.2 copy.43
  479.1 18.6 %convolution_bitcast_fusion = f32[8,256,20,128]{1,3,0,2:T(8,128)S(1)} fusion(f32[256,20,128]{2,0,1:T(8,128)} %copy.43, f32[256,20,128]{2,0,1:T(8,128)S(1)} %copy.42, f32[8]{0:T(128)S(1)} %multiply_rsqrt_fusion, s32[8]{0:T(128)S(1)} %copy-done.14), kind=kOutput, calls=%fused_computation | convolution fusion | flops 16108748800 | bytes 26214464 | tf_op jit(solution)/shard_map/rbj,jk->rbk/dot_general | solution.py:96
  497.7 7.4 %copy.35 = f32[8,256,20,128]{1,3,2,0:T(8,128)} copy(f32[8,256,20,128]{1,3,0,2:T(8,128)S(1)} %convolution_bitcast_fusion) | data formatting | bytes 41943040 | tf_op jit(solution)/shard_map/transpose | solution.py:98
  505.2 19.9 %copy.36 = f32[8,256,2560]{2,1,0:T(8,128)} copy(f32[8,256,2560]{1,2,0:T(8,128)} %bitcast.83) | data formatting | bytes 41943040 | tf_op jit(solution)/shard_map/reshape | solution.py:98
  (188 shorter events, 122.8 us)
Async XLA Ops:
  1.0 5.6 %collective-permute-start = (f32[256,255]{1,0:T(8,128)S(1)}, f32[256,255]{1,0:T(8,128)S(1)}, u32[]{:S(2)}, u32[]{:S(2)}) collective-permute-start(f32[256,255]{1,0:T(8,128)S(1)} %slice.507), channel_id=1, source_target_pairs={{1,0},{3,2},{5,4},{7,6},{9,8},{11,10},{13,12},{15,14},{17,16},{19,... | collective-permute-start | bytes 783368 | tf_op jit(solution)/shard_map/ppermute | solution.py:13
  21.0 3.1 copy-start.6
  55.0 4.6 copy-start.4
  83.5 1.8 copy-start.5
  117.7 0.7 copy-start.11
  118.4 0.6 copy-start.10
  119.0 0.7 copy-start.9
  120.2 5.5 %copy-start.12 = (pred[256]{0:T(512)(128)(4,1)S(1)}, pred[256]{0:T(512)(128)(4,1)}, u32[]{:S(2)}) copy-start(pred[256]{0:T(512)(128)(4,1)} %get-tuple-element.14) | copy-start | bytes 772
  120.2 5.5 %copy-start.13 = (pred[256]{0:T(512)(128)(4,1)S(1)}, pred[256]{0:T(512)(128)(4,1)}, u32[]{:S(2)}) copy-start(pred[256]{0:T(512)(128)(4,1)} %get-tuple-element.101) | copy-start | bytes 772
  126.7 71.3 %copy-start.2 = (f32[256,2560]{0,1:T(8,128)}, f32[256,2560]{0,1:T(8,128)S(1)}, u32[]{:S(2)}) copy-start(f32[256,2560]{0,1:T(8,128)S(1)} %bitcast_add_fusion) | copy-start | bytes 7864324
  126.8 8.2 %copy-start.8 = (s32[1,256]{1,0:T(1,128)S(1)}, s32[1,256]{1,0:T(1,128)}, u32[]{:S(2)}) copy-start(s32[1,256]{1,0:T(1,128)} %get-tuple-element.119) | copy-start | bytes 3076
  126.8 3.4 collective-permute-start.1
  132.0 66.1 %collective-permute-start.2 = (f32[256,2816]{0,1:T(8,128)}, f32[256,2816]{0,1:T(8,128)}, u32[]{:S(2)}, u32[]{:S(2)}) collective-permute-start(f32[256,2816]{0,1:T(8,128)} %pad_maximum_fusion.3), channel_id=1, source_target_pairs={{0,2},{2,0},{4,6},{6,4},{8,10},{10,8},{12,14},{14,12},{1,3},{3,1},... | collective-permute-start | bytes 8650760 | tf_op jit(solution)/shard_map/ppermute | solution.py:19
  201.9 1.7 copy-start.3
  206.4 76.2 %copy-start = (f32[256,2560]{0,1:T(8,128)}, f32[256,2560]{0,1:T(8,128)S(1)}, u32[]{:S(2)}) copy-start(f32[256,2560]{0,1:T(8,128)S(1)} %fusion.13) | copy-start | bytes 7864324
  206.5 3.8 collective-permute-start.3
  212.1 70.5 %collective-permute-start.4 = (f32[256,3072]{0,1:T(8,128)}, f32[256,3072]{0,1:T(8,128)}, u32[]{:S(2)}, u32[]{:S(2)}) collective-permute-start(f32[256,3072]{0,1:T(8,128)} %pad_maximum_fusion.1), channel_id=1, source_target_pairs={{0,4},{2,6},{4,0},{6,2},{8,12},{10,14},{12,8},{14,10},{1,5},{3,7},... | collective-permute-start | bytes 9437192 | tf_op jit(solution)/shard_map/ppermute | solution.py:19
  287.0 1.7 copy-start.1
  291.6 4.6 collective-permute-start.5
  296.1 2.2 copy-start.7
  298.3 160.5 %collective-permute-start.6 = (f32[256,3584]{0,1:T(8,128)}, f32[256,3584]{0,1:T(8,128)}, u32[]{:S(2)}, u32[]{:S(2)}) collective-permute-start(f32[256,3584]{0,1:T(8,128)} %pad_maximum_fusion), channel_id=1, source_target_pairs={{0,8},{2,10},{4,12},{6,14},{8,0},{10,2},{12,4},{14,6},{1,9},{3,11}... | collective-permute-start | bytes 11010056 | tf_op jit(solution)/shard_map/ppermute | solution.py:19
  464.6 4.1 copy-start.14
  467.4 3.2 collective-permute-start.7
where the time goes:
time: 535 us; the launch traced here: 525 us
  waiting for transfers between devices  298 us (56%)
  local copies, waits for them, and re-layouts  124 us (23%)
  other arithmetic  69.2 us (13%)
  matrix products  18.6 us (3%)
  starting transfers between devices  14.5 us (3%)
    ppermute x3, waiting for transfers between devices, from_partner(): return lax.ppermute(value, axis, pairs)  289 us
    add x19, local copies, waits for them, and re-layouts, delay_block(): block_view[:, 0, :, :out_width][:, None]  26 us
    select_n x45, other arithmetic, delay_rows(): jnp.where(chosen, result[:, bit_value:], result[:, :width_now - bit_value])  20.9 us
    reshape x1, local copies, waits for them, and re-layouts, local(): jnp.transpose(product, (2, 0, 1, 3))  19.9 us
    dot_general x1, matrix products, local(): jnp.einsum('rbj,jk->rbk', paired, filter_matrix, precision=lax.Precision....  18.6 us
    broadcast_in_dim x17, local copies, waits for them, and re-layouts, delay_block(): jnp.broadcast_to(block_view[:, 1][:, None], (group_count, 2, half_rows, t...  16.8 us
    select_n x7, other arithmetic, delay_rows(): return jnp.where(shift_col == top_reach, top_shift, lower_shift)  12.1 us
  transfers between devices with their start and end apart: 8, of which 7 were waited for; matrix products, arithmetic and copies ran while one was open for 1% of the time, Pallas kernels for 0%

commit v1 on v0

v1 whole, which is shorter than its diff:
```python
import functools

import jax
import jax.numpy as jnp
from jax import lax
from jax.experimental import pallas as pl
from jax.experimental.pallas import tpu as pltpu
from jax.sharding import PartitionSpec as P

LANES = 128
SUB = 8
TAPS = 128
VMEM = pltpu.MemorySpace.VMEM
SMEM = pltpu.MemorySpace.SMEM


def cdiv(a, b):
    return -(-a // b)


def lane_shift(low, high, shift, lane):
    picked = jnp.where(lane < shift, high, low)
    return jnp.take_along_axis(
        picked, (lane + shift) & (LANES - 1), axis=1, mode="promise_in_bounds"
    )


def local_tree_kernel(levels, blocks, lead_blocks, own, spectra, lead, shifts, out, buf_a, buf_b):
    rows = spectra.shape[0]
    lane = lax.broadcasted_iota(jnp.int32, (SUB, LANES), 1)
    sub = lax.broadcasted_iota(jnp.int32, (SUB, LANES), 0)

    def out_blocks(level):
        return blocks + cdiv(2**levels - 2 ** (level + 1), LANES)

    def shift_of(group, level):
        col = shifts[pl.ds(group * SUB, SUB), level : level + 1]
        return jnp.broadcast_to(col, (SUB, LANES))

    def first_levels(group, carry):
        at = pl.ds(pl.multiple_of(group * SUB, SUB), SUB)
        x = [spectra[at, b * LANES : (b + 1) * LANES] for b in range(blocks)]
        x += [lead[at, b * LANES : (b + 1) * LANES] for b in range(lead_blocks)]
        for level in range(3):
            h = 2**level
            shift = shift_of(group, level)
            upper = (sub & h) != 0
            b_rows = [jnp.where(upper, v, pltpu.roll(v, SUB - h, 0)) for v in x]
            nxt = []
            for b in range(out_blocks(level)):
                a_rows = jnp.where(upper, pltpu.roll(x[b], h, 0), x[b])
                high = b_rows[min(b + 1, len(x) - 1)]
                nxt.append(a_rows + lane_shift(b_rows[b], high, shift, lane))
            x = nxt
        for b, v in enumerate(x):
            buf_a[b, at, :] = v
        return carry

    lax.fori_loop(0, rows // SUB, first_levels, 0)

    def store(dst, last, b, group, value):
        if not last:
            dst[b, pl.ds(pl.multiple_of(group * SUB, SUB), SUB), :] = value
        elif own % SUB == 0:
            per = own // SUB
            dst[group // per, b, pl.ds(pl.multiple_of((group % per) * SUB, SUB), SUB), :] = value
        else:
            for r in range(SUB):
                dst[group * (SUB // own) + r // own, b, r % own : r % own + 1, :] = value[r : r + 1]

    src, dst = buf_a, buf_b
    for level in range(3, levels):
        last = level == levels - 1
        target = out if last else dst
        hg = 2**level // SUB
        in_count = out_blocks(level - 1)
        count = out_blocks(level)

        def pair(p, carry, src=src, target=target, hg=hg, count=count, in_count=in_count, last=last, level=level):
            g_a = (p // hg) * (2 * hg) + p % hg
            g_b = g_a + hg
            at_a = pl.ds(pl.multiple_of(g_a * SUB, SUB), SUB)
            at_b = pl.ds(pl.multiple_of(g_b * SUB, SUB), SUB)
            s_a, s_b = shift_of(g_a, level), shift_of(g_b, level)
            low = src[0, at_b, :]
            for b in range(count):
                high = src[b + 1, at_b, :] if b + 1 < in_count else low
                a = src[b, at_a, :]
                store(target, last, b, g_a, a + lane_shift(low, high, s_a, lane))
                store(target, last, b, g_b, a + lane_shift(low, high, s_b, lane))
                low = high
            return carry

        lax.fori_loop(0, rows // (2 * SUB), pair, 0)
        src, dst = dst, src


def local_tree(spectra, lead, shifts, parts):
    rows, span = spectra.shape
    levels = rows.bit_length() - 1
    blocks = span // LANES
    lead_blocks = lead.shape[1] // LANES
    own = rows // parts
    spec = pl.BlockSpec(memory_space=VMEM)
    buf = pltpu.VMEM((blocks + lead_blocks, rows, LANES), jnp.float32)
    return pl.pallas_call(
        functools.partial(local_tree_kernel, levels, blocks, lead_blocks, own),
        out_shape=jax.ShapeDtypeStruct((parts, blocks, own, LANES), jnp.float32),
        in_specs=[spec] * 3,
        out_specs=spec,
        scratch_shapes=[buf, buf],
    )(spectra, lead, shifts)


def cross_rows(src, dst, shifts, level, bits, own, first, count, in_pitch, out_pitch, windows, width):
    lane = lax.broadcasted_iota(jnp.int32, (width, LANES), 1)
    bands = 2**bits
    step = 2**level

    def one_row(i, carry):
        for j in range(bands):
            base = (j // (2 * step)) * (2 * step) + j % step
            shift = shifts[(level * bands + j) * own + i]
            block = shift // LANES
            rest = shift % LANES
            for w, (start, out_start) in enumerate(windows):
                a = src[pl.ds((base * in_pitch + start) * own + i, width, stride=own), :]
                b_at = ((base + step) * in_pitch + start + block) * own + i
                low = src[pl.ds(b_at, width, stride=own), :]
                high = src[pl.ds(b_at + own, width, stride=own), :]
                moved = pltpu.roll(jnp.where(lane < rest, high, low), (LANES - rest) % LANES, 1)
                dst[pl.ds((j * out_pitch + out_start) * own + i, width, stride=own), :] = a + moved
        return carry

    lax.fori_loop(first, first + count, one_row, 0)


def cross_kernel(bits, own, blocks, halves, pitch, shifts, arrived, out, buf_a, buf_b, sem):
    total = blocks * halves
    bands = 2**bits
    copies = []
    for s in range(bands):
        c = pltpu.make_async_copy(
            arrived.at[pl.ds(s * total * own, total * own), :],
            buf_a.at[pl.ds(s * pitch * own, total * own), :],
            sem.at[s],
        )
        c.start()
        copies.append(c)
    zero = jnp.zeros(((pitch - total) * own, LANES), jnp.float32)
    for s in range(bands):
        for buf in (buf_a, buf_b):
            buf[pl.ds((s * pitch + total) * own, (pitch - total) * own), :] = zero
    for c in copies:
        c.wait()
    src, dst = buf_a, buf_b
    for level in range(bits):
        if level < bits - 1:
            cross_rows(src, dst, shifts, level, bits, own, 0, own, pitch, pitch, [(0, 0)], total)
        else:
            out_blocks = blocks + 1
            windows = [(c * blocks, c * out_blocks) for c in range(halves)]
            cross_rows(src, out, shifts, level, bits, own, 0, own, pitch, halves * out_blocks, windows, out_blocks)
        src, dst = dst, src


def cross_tree(arrived, shifts, bits, own, blocks, halves, reach):
    bands = 2**bits
    pitch = blocks * halves + cdiv(reach, LANES) + 2
    buf = pltpu.VMEM((bands * pitch * own, LANES), jnp.float32)
    return pl.pallas_call(
        functools.partial(cross_kernel, bits, own, blocks, halves, pitch),
        out_shape=jax.ShapeDtypeStruct((bands * halves * (blocks + 1) * own, LANES), jnp.float32),
        in_specs=[pl.BlockSpec(memory_space=SMEM), pl.BlockSpec(memory_space=pl.ANY)],
        out_specs=pl.BlockSpec(memory_space=VMEM),
        scratch_shapes=[buf, buf, pltpu.SemaphoreType.DMA((bands,))],
    )(shifts, arrived)


def filter_kernel(per_step, widths, scaling, x, out, matrix):
    filters, rows, _ = out.shape

    @pl.when(pl.program_id(0) == 0)
    def _():
        pos = lax.broadcasted_iota(jnp.int32, (2 * TAPS, TAPS), 0)
        dist = pos - lax.broadcasted_iota(jnp.int32, (2 * TAPS, TAPS), 1)
        for w in range(filters):
            box = (dist >= 0) & (dist < widths[w])
            matrix[:, w * TAPS : (w + 1) * TAPS] = jnp.where(box, 1.0, 0.0).astype(jnp.bfloat16)

    first = pl.program_id(0) * per_step
    for k in range(per_step):
        b = first + k
        parts = [x[:, b + n, :, :].reshape(rows, LANES) for n in range(2)]
        rows_in = jnp.concatenate(parts, axis=1)
        head = rows_in.astype(jnp.bfloat16)
        tail = (rows_in - head.astype(jnp.float32)).astype(jnp.bfloat16)
        for w in range(filters):
            m = matrix[:, w * TAPS : (w + 1) * TAPS]
            y = jnp.dot(head, m, preferred_element_type=jnp.float32)
            y += jnp.dot(tail, m, preferred_element_type=jnp.float32)
            out[w, :, k * LANES : (k + 1) * LANES] = y * scaling[w]


def filter_rows(x, widths, scaling, rows):
    filters = widths.shape[0]
    blocks = x.shape[1] - 1
    per_step = 2 if blocks % 2 == 0 else 1
    if x.shape[2] % SUB:
        x = jnp.transpose(x, (1, 0, 2, 3)).reshape(1, blocks + 1, rows, LANES)
    return pl.pallas_call(
        functools.partial(filter_kernel, per_step),
        grid=(blocks // per_step,),
        out_shape=jax.ShapeDtypeStruct((filters, rows, blocks * LANES), jnp.float32),
        in_specs=[
            pl.BlockSpec(memory_space=SMEM),
            pl.BlockSpec(memory_space=SMEM),
            pl.BlockSpec(memory_space=VMEM),
        ],
        out_specs=pl.BlockSpec((filters, rows, per_step * LANES), lambda s: (0, 0, s)),
        scratch_shapes=[pltpu.VMEM((2 * TAPS, filters * TAPS), jnp.bfloat16)],
    )(widths, scaling, x)


def local(spectra, delays, widths):
    rows, span = spectra.shape
    all_levels, all_rows = delays.shape
    levels = rows.bit_length() - 1
    bits = all_levels - levels
    bands, halves = lax.axis_size("freq"), lax.axis_size("tm")
    parts = bands * halves
    own = rows // parts
    blocks = span // LANES
    lead_width = cdiv(rows - 1, LANES) * LANES
    position = lax.axis_index("freq")
    lead = lax.ppermute(spectra[:, :lead_width], "tm", [(k, k - 1) for k in range(1, halves)])
    own_shifts = lax.dynamic_slice_in_dim(delays[:levels], position * rows, rows, 1).T
    x = local_tree(spectra, lead, own_shifts, parts)
    x = lax.all_to_all(x, ("freq", "tm"), 0, 0, tiled=True)
    mine = (position * halves + lax.axis_index("tm")) * own
    shifts = lax.dynamic_slice_in_dim(delays[levels:].reshape(bits, bands, rows), mine, own, 2)
    x = cross_tree(
        x.reshape(-1, LANES), shifts.reshape(-1), bits, own, blocks, halves, 2 ** (all_levels - 1)
    )
    x = x.reshape(parts, blocks + 1, own, LANES)
    x = lax.all_to_all(x, ("freq", "tm"), 0, 0, tiled=True)
    scaling = 1.0 / jnp.sqrt(widths.astype(jnp.float32) * all_rows)
    return filter_rows(x, widths, scaling, rows)


def solution(mesh):
    return jax.shard_map(
        local,
        mesh=mesh,
        in_specs=(P(("beam", "freq"), "tm"), P(), P()),
        out_specs=P(None, ("beam", "freq"), "tm"),
        check_vma=False,
    )
```

time: 535 us -> 206 us (0.39)
  the two profiles are of different devices: /device:TPU:0 before, /device:TPU:15 now
where the time goes in v1:
time: 206 us; the launch traced here: 205 us
  waiting for transfers between devices  119 us (58%)
  Pallas kernels  65.2 us (32%)
  starting transfers between devices  13.5 us (7%)
  local copies, waits for them, and re-layouts  7.15 us (3%)
    all_to_all x2, waiting for transfers between devices, local(): x = lax.all_to_all(x, ('freq', 'tm'), 0, 0, tiled=True)  119 us
    pallas_call x1, Pallas kernels, local_tree(): pl.pallas_call(functools.partial(local_tree_kernel, levels, blocks, lead_...  32 us
    pallas_call x1, Pallas kernels, cross_tree(): pl.pallas_call(functools.partial(cross_kernel, bits, own, blocks, halves,...  17.1 us
    pallas_call x1, Pallas kernels, filter_rows(): pl.pallas_call(functools.partial(filter_kernel, per_step), grid=(blocks /...  16.1 us
    all_to_all x2, starting transfers between devices, local(): x = lax.all_to_all(x, ('freq', 'tm'), 0, 0, tiled=True)  10.9 us
    unnamed x10, local copies, waits for them, and re-layouts  4.58 us
  transfers between devices with their start and end apart: 3, of which 2 were waited for; matrix products, arithmetic and copies ran while one was open for 1% of the time, Pallas kernels for 0%

profile of v1, /device:TPU:15, one launch (start us, length us, event | category | flops | bytes accessed | tf_op | source)
XLA Modules:
  0.0 205.2 jit_solution(15840728712927249856)
XLA Ops:
  0.0 1.0 slice.10
  1.0 2.6 %collective-permute-start = (f32[256,256]{1,0:T(8,128)S(1)}, f32[256,256]{1,0:T(8,128)S(1)}, u32[]{:S(2)}, u32[]{:S(2)}) collective-permute-start(f32[256,256]{1,0:T(8,128)S(1)} %slice.10), channel_id=1, source_target_pairs={{1,0},{3,2},{5,4},{7,6},{9,8},{11,10},{13,12},{15,14},{17,16},{19,... | collective-permute-start | bytes 786440 | tf_op jit(solution)/shard_map/ppermute | solution.py:236
  3.6 0.8 slice.11
  4.4 0.8 copy.5
  5.2 0.0 collective-permute-done.lead
  5.2 0.0 copy-start.2
  5.2 0.7 copy-done.2
  5.9 32.0 %shard_map.37 = f32[16,20,16,128]{3,2,1,0:T(8,128)} custom-call(f32[256,2560]{1,0:T(8,128)} %spectra.1, f32[256,256]{1,0:T(8,128)} %copy-done.2, s32[256,8]{1,0:T(8,128)} %bitcast.9), custom_call_target="tpu_custom_call" | custom-call | tf_op jit(solution)/shard_map/pallas_call | solution.py:106
  38.0 0.0 slice-start
  38.0 6.1 %all-to-all-start = ((f32[16,20,16,128]{3,2,1,0:T(8,128)}), f32[16,20,16,128]{3,2,1,0:T(8,128)S(1)}, u32[]{:S(2)}, u32[]{:S(2)}) async-start(f32[16,20,16,128]{3,2,1,0:T(8,128)} %shard_map.37), calls=%async_computation | async-start | bytes 5242880 | tf_op jit(solution)/shard_map/all_to_all | solution.py:239
  44.1 0.0 slice-done
  44.1 0.1 constant_dynamic-slice_fusion.1
  44.2 0.7 reshape.13.shifts
  44.8 57.9 %all-to-all-done = f32[16,20,16,128]{3,2,1,0:T(8,128)S(1)} async-done(((f32[16,20,16,128]{3,2,1,0:T(8,128)}), f32[16,20,16,128]{3,2,1,0:T(8,128)S(1)}, u32[]{:S(2)}, u32[]{:S(2)}) %all-to-all-start) | async-done | bytes 2621472 | tf_op jit(solution)/shard_map/all_to_all | solution.py:239
  102.7 0.0 copy-start.1
  102.7 1.5 copy-done.1
  104.2 17.1 %shard_map.38 = f32[5376,128]{1,0:T(8,128)} custom-call(s32[384]{0:T(512)} %reshape.13.shifts, f32[5120,128]{1,0:T(8,128)} %bitcast.8), custom_call_target="tpu_custom_call" | custom-call | tf_op jit(solution)/shard_map/pallas_call | solution.py:171
  121.3 0.0 copy-start.3
  121.3 4.8 %all-to-all-start.1 = ((f32[16,21,16,128]{3,2,1,0:T(8,128)}), f32[16,21,16,128]{3,2,1,0:T(8,128)S(1)}, u32[]{:S(2)}, u32[]{:S(2)}) async-start(f32[16,21,16,128]{3,2,1,0:T(8,128)} %bitcast.7), calls=%async_computation.1 | async-start | bytes 5505024 | tf_op jit(solution)/shard_map/all_to_all | solution.py:246
  126.1 0.0 copy-done.3
  126.1 0.5 multiply_rsqrt_fusion.scaling
  126.7 60.9 %all-to-all-done.1.x = f32[16,21,16,128]{3,2,1,0:T(8,128)S(1)} async-done(((f32[16,21,16,128]{3,2,1,0:T(8,128)}), f32[16,21,16,128]{3,2,1,0:T(8,128)S(1)}, u32[]{:S(2)}, u32[]{:S(2)}) %all-to-all-start.1) | async-done | bytes 2752544 | tf_op jit(solution)/shard_map/all_to_all | solution.py:246
  187.6 1.5 copy-done
  189.1 16.1 %shard_map.39 = f32[8,256,2560]{2,1,0:T(8,128)} custom-call(s32[8]{0:T(128)} %widths.1, f32[8]{0:T(128)} %multiply_rsqrt_fusion.scaling, f32[16,21,16,128]{3,2,1,0:T(8,128)} %copy-done), custom_call_target="tpu_custom_call" | custom-call | tf_op jit(solution)/shard_map/pallas_call | solution.py:211
  (3 shorter events, 0.0 us)
Async XLA Ops:
  1.0 4.3 %collective-permute-start = (f32[256,256]{1,0:T(8,128)S(1)}, f32[256,256]{1,0:T(8,128)S(1)}, u32[]{:S(2)}, u32[]{:S(2)}) collective-permute-start(f32[256,256]{1,0:T(8,128)S(1)} %slice.10), channel_id=1, source_target_pairs={{1,0},{3,2},{5,4},{7,6},{9,8},{11,10},{13,12},{15,14},{17,16},{19,... | collective-permute-start | bytes 786440 | tf_op jit(solution)/shard_map/ppermute | solution.py:236
  5.2 0.7 copy-start.2
  38.0 6.1 %slice-start = ((s32[11,2048]{1,0:T(8,128)}), s32[3,2048]{1,0:T(4,128)S(1)}, s32[]{:S(2)}) async-start(s32[11,2048]{1,0:T(8,128)} %param.4), calls=%async_computation.2 | async-start | bytes 65536 | tf_op jit(solution)/shard_map/slice | solution.py:241
  38.0 64.7 %all-to-all-start = ((f32[16,20,16,128]{3,2,1,0:T(8,128)}), f32[16,20,16,128]{3,2,1,0:T(8,128)S(1)}, u32[]{:S(2)}, u32[]{:S(2)}) async-start(f32[16,20,16,128]{3,2,1,0:T(8,128)} %shard_map.37), calls=%async_computation | async-start | bytes 5242880 | tf_op jit(solution)/shard_map/all_to_all | solution.py:239
  102.7 1.5 copy-start.1
  121.3 4.8 %copy-start.3 = (s32[8]{0:T(128)S(1)}, s32[8]{0:T(128)}, u32[]{:S(2)}) copy-start(s32[8]{0:T(128)} %widths.1) | copy-start | bytes 100
  121.3 66.3 %all-to-all-start.1 = ((f32[16,21,16,128]{3,2,1,0:T(8,128)}), f32[16,21,16,128]{3,2,1,0:T(8,128)S(1)}, u32[]{:S(2)}, u32[]{:S(2)}) async-start(f32[16,21,16,128]{3,2,1,0:T(8,128)} %bitcast.7), calls=%async_computation.1 | async-start | bytes 5505024 | tf_op jit(solution)/shard_map/all_to_all | solution.py:246
  187.6 1.5 copy-start

commit v2 on v0

v2 whole, which is shorter than its diff:
```python
import functools

import jax
import jax.numpy as jnp
from jax import lax
from jax.experimental import pallas as pl
from jax.experimental.pallas import tpu as pltpu
from jax.sharding import PartitionSpec as P

LANES = 128
SUB = 8
TAPS = 128
VMEM = pltpu.MemorySpace.VMEM
SMEM = pltpu.MemorySpace.SMEM


def cdiv(a, b):
    return -(-a // b)


def round_up(a, b):
    return cdiv(a, b) * b


def shifted(src, start, width, shift, reach, lane):
    if reach >= LANES:
        start = start + shift // LANES
        shift = shift % LANES
    low = src[pl.ds(start, width), :]
    high = src[pl.ds(start + 1, width), :]
    return pltpu.roll(jnp.where(lane < shift, high, low), (LANES - shift) % LANES, 1)


def local_tree_kernel(levels, blocks, lead_blocks, own, pitch, spectra, lead, shifts, *refs):
    *outs, buf_a, buf_b = refs
    rows = spectra.shape[0]
    groups = len(outs)
    per = own // groups
    lane = lax.broadcasted_iota(jnp.int32, (pitch, LANES), 1)
    out_lane = lax.broadcasted_iota(jnp.int32, (blocks, LANES), 1)

    def spread(group, carry):
        at = pl.ds(pl.multiple_of(group * SUB, SUB), SUB)
        for b in range(blocks + lead_blocks):
            if b < blocks:
                v = spectra[at, b * LANES : (b + 1) * LANES]
            else:
                v = lead[at, (b - blocks) * LANES : (b - blocks + 1) * LANES]
            buf_a[pl.ds(group * (SUB * pitch) + b, SUB, stride=pitch), :] = v
        return carry

    lax.fori_loop(0, rows // SUB, spread, 0)

    src, dst = buf_a, buf_b
    for level in range(levels - 1):
        half = 2**level
        unroll = 4

        def pairs(n, carry, src=src, dst=dst, half=half, level=level):
            for u in range(unroll):
                p = n * unroll + u
                row_a = (p // half) * (2 * half) + p % half
                at_a = pl.multiple_of(row_a * pitch, SUB)
                at_b = pl.multiple_of((row_a + half) * pitch, SUB)
                a = src[pl.ds(at_a, pitch), :]
                for e, at in enumerate((at_a, at_b)):
                    shift = shifts[level * rows + row_a + e * half]
                    dst[pl.ds(at, pitch), :] = a + shifted(src, at_b, pitch, shift, half, lane)
            return carry

        lax.fori_loop(0, rows // 2 // unroll, pairs, 0)
        src, dst = dst, src

    level = levels - 1
    half = 2**level
    for group, out in enumerate(outs):
        unroll = 4

        def last_pairs(n, carry, src=src, out=out, group=group):
            for u in range(unroll):
                m = n * unroll + u
                row_a = (m // per) * own + group * per + m % per
                at_a = pl.multiple_of(row_a * pitch, SUB)
                at_b = pl.multiple_of((row_a + half) * pitch, SUB)
                a = src[pl.ds(at_a, blocks), :]
                for e in range(2):
                    row = row_a + e * half
                    shift = shifts[level * rows + row]
                    at = ((row // own) * per + m % per) * blocks
                    out[pl.ds(at, blocks), :] = a + shifted(src, at_b, blocks, shift, half, out_lane)
            return carry

        lax.fori_loop(0, rows // 2 // groups // unroll, last_pairs, 0)


def local_tree(spectra, lead, shifts, parts, groups):
    rows, span = spectra.shape
    levels = rows.bit_length() - 1
    blocks = span // LANES
    lead_blocks = lead.shape[1] // LANES
    own = rows // parts
    pitch = round_up(blocks + lead_blocks, SUB)
    spec = pl.BlockSpec(memory_space=VMEM)
    buf = pltpu.VMEM((rows * pitch + SUB, LANES), jnp.float32)
    shape = jax.ShapeDtypeStruct((rows // groups * blocks, LANES), jnp.float32)
    return pl.pallas_call(
        functools.partial(local_tree_kernel, levels, blocks, lead_blocks, own, pitch),
        out_shape=[shape] * groups,
        in_specs=[spec, spec, pl.BlockSpec(memory_space=SMEM)],
        out_specs=[spec] * groups,
        scratch_shapes=[buf, buf],
    )(spectra, lead, shifts)


def cross_kernel(bits, rows, own, first, blocks, halves, pitch, first_level, shifts, arrived, out, buf_a, buf_b):
    total = blocks * halves
    bands = 2**bits
    out_blocks = blocks + 1
    lane = lax.broadcasted_iota(jnp.int32, (total, LANES), 1)
    out_lane = lax.broadcasted_iota(jnp.int32, (out_blocks, LANES), 1)
    zero = jnp.zeros((pitch - total, LANES), jnp.float32)

    def gather(i, carry):
        for s in range(bands):
            at = (s * rows + i) * pitch
            for c in range(halves):
                piece = arrived[pl.ds(((s * halves + c) * rows + i) * blocks, blocks), :]
                buf_a[pl.ds(at + c * blocks, blocks), :] = piece
            for buf in (buf_a, buf_b):
                buf[pl.ds(at + total, pitch - total), :] = zero
        return carry

    lax.fori_loop(0, rows, gather, 0)

    src, dst = buf_a, buf_b
    for level in range(bits):
        step = 2**level
        reach = 2 ** (first_level + level)

        def one_row(i, carry, src=src, dst=dst, step=step, level=level, reach=reach):
            for j in range(bands):
                base = (j // (2 * step)) * (2 * step) + j % step
                shift = shifts[(level * bands + j) * own + first + i]
                at_a = pl.multiple_of((base * rows + i) * pitch, SUB)
                at_b = pl.multiple_of(((base + step) * rows + i) * pitch, SUB)
                if level < bits - 1:
                    a = src[pl.ds(at_a, total), :]
                    at = pl.multiple_of((j * rows + i) * pitch, SUB)
                    dst[pl.ds(at, total), :] = a + shifted(src, at_b, total, shift, reach, lane)
                    continue
                for c in range(halves):
                    a = src[pl.ds(at_a + c * blocks, out_blocks), :]
                    moved = shifted(src, at_b + c * blocks, out_blocks, shift, reach, out_lane)
                    out[pl.ds(((j * halves + c) * rows + i) * out_blocks, out_blocks), :] = a + moved
            return carry

        lax.fori_loop(0, rows, one_row, 0)
        src, dst = dst, src


def cross_tree(arrived, shifts, bits, own, group, groups, blocks, halves, first_level):
    bands = 2**bits
    reach = 2 ** (first_level + bits - 1)
    pitch = round_up(blocks * halves + cdiv(reach, LANES) + 2, SUB)
    rows = own // groups
    buf = pltpu.VMEM((bands * rows * pitch + SUB, LANES), jnp.float32)
    out_rows = bands * halves * (blocks + 1) * rows
    return pl.pallas_call(
        functools.partial(
            cross_kernel, bits, rows, own, group * rows, blocks, halves, pitch, first_level
        ),
        out_shape=jax.ShapeDtypeStruct((out_rows, LANES), jnp.float32),
        in_specs=[pl.BlockSpec(memory_space=SMEM), pl.BlockSpec(memory_space=VMEM)],
        out_specs=pl.BlockSpec(memory_space=VMEM),
        scratch_shapes=[buf, buf],
        cost_estimate=pl.CostEstimate(flops=0, bytes_accessed=20 * out_rows * LANES, transcendentals=0),
    )(shifts, arrived)


def filter_kernel(per_step, blocks, filters, widths, scaling, x, *refs):
    out, matrix = refs[-2:]
    rows = out.shape[1] * out.shape[2]

    @pl.when(pl.program_id(0) == 0)
    def _():
        pos = lax.broadcasted_iota(jnp.int32, (2 * TAPS, TAPS), 0)
        dist = pos - lax.broadcasted_iota(jnp.int32, (2 * TAPS, TAPS), 1)
        for w in range(filters):
            box = (dist >= 0) & (dist < widths[w])
            value = jnp.where(box, 1.0, 0.0).astype(jnp.bfloat16)
            for n in range(2):
                matrix[n * 2 * TAPS : (n + 1) * 2 * TAPS, w * TAPS : (w + 1) * TAPS] = value

    first = pl.program_id(0) * per_step
    pieces = [x[pl.ds(first + n, rows, stride=blocks + 1), :] for n in range(per_step + 1)]
    heads = [v.astype(jnp.bfloat16) for v in pieces]
    tails = [(v - h.astype(jnp.float32)).astype(jnp.bfloat16) for v, h in zip(pieces, heads)]
    together = 2 if filters % 2 == 0 else 1
    for k in range(per_step):
        lhs = jnp.concatenate([heads[k], heads[k + 1], tails[k], tails[k + 1]], axis=1)
        for w in range(0, filters, together):
            m = matrix[:, w * TAPS : (w + together) * TAPS]
            y = jnp.dot(lhs, m, preferred_element_type=jnp.float32)
            for n in range(together):
                part = y[:, n * TAPS : (n + 1) * TAPS] * scaling[w + n]
                out[w + n, :, :, k * LANES : (k + 1) * LANES] = part.reshape(out.shape[1], out.shape[2], LANES)


def filter_rows(x, into, widths, scaling, parts, own, group, groups, blocks):
    filters = widths.shape[0]
    per_step = 2 if blocks % 2 == 0 else 1
    rows = own // groups
    if rows % SUB:
        view, block, where = (filters, 1, parts * own), (filters, 1, parts * own), (0, 0, 0)
    else:
        view, block, where = (filters, parts, own), (filters, parts, rows), (0, 0, group)
    specs = [
        pl.BlockSpec(memory_space=SMEM),
        pl.BlockSpec(memory_space=SMEM),
        pl.BlockSpec(memory_space=VMEM),
    ]
    args = [widths, scaling, x]
    if into is not None:
        specs.append(pl.BlockSpec(memory_space=pl.ANY))
        args.append(into)
    cells = filters * parts * rows * blocks * LANES
    return pl.pallas_call(
        functools.partial(filter_kernel, per_step, blocks, filters),
        grid=(blocks // per_step,),
        out_shape=jax.ShapeDtypeStruct(view + (blocks * LANES,), jnp.float32),
        in_specs=specs,
        out_specs=pl.BlockSpec(block + (per_step * LANES,), lambda s: where + (s,)),
        scratch_shapes=[pltpu.VMEM((4 * TAPS, filters * TAPS), jnp.bfloat16)],
        input_output_aliases={} if into is None else {3: 0},
        cost_estimate=pl.CostEstimate(flops=1024 * cells, bytes_accessed=4 * cells, transcendentals=0),
    )(*args)


GROUPS = 2


def local(spectra, delays, widths):
    rows, span = spectra.shape
    all_levels, all_rows = delays.shape
    levels = rows.bit_length() - 1
    bits = all_levels - levels
    bands, halves = lax.axis_size("freq"), lax.axis_size("tm")
    parts = bands * halves
    own = rows // parts
    groups = GROUPS if own % (SUB * GROUPS) == 0 else 1
    blocks = span // LANES
    lead_width = cdiv(rows - 1, LANES) * LANES
    position = lax.axis_index("freq")
    lead = lax.ppermute(spectra[:, :lead_width], "tm", [(k, k - 1) for k in range(1, halves)])
    own_shifts = lax.dynamic_slice_in_dim(delays[:levels], position * rows, rows, 1).reshape(-1)
    mine = (position * halves + lax.axis_index("tm")) * own
    shifts = lax.dynamic_slice_in_dim(delays[levels:].reshape(bits, bands, rows), mine, own, 2)
    shifts = shifts.reshape(-1)
    scaling = 1.0 / jnp.sqrt(widths.astype(jnp.float32) * all_rows)

    def turn(x):
        x = x.reshape(parts, -1, LANES)
        return lax.all_to_all(x, ("freq", "tm"), 0, 0, tiled=True).reshape(-1, LANES)

    sections = [turn(x) for x in local_tree(spectra, lead, own_shifts, parts, groups)]
    rows_done = [
        turn(cross_tree(x, shifts, bits, own, g, groups, blocks, halves, levels))
        for g, x in enumerate(sections)
    ]
    filtered = None
    for g, x in enumerate(rows_done):
        filtered = filter_rows(x, filtered, widths, scaling, parts, own, g, groups, blocks)
    return filtered.reshape(widths.shape[0], rows, span)


def solution(mesh):
    return jax.shard_map(
        local,
        mesh=mesh,
        in_specs=(P(("beam", "freq"), "tm"), P(), P()),
        out_specs=P(None, ("beam", "freq"), "tm"),
        check_vma=False,
    )
```

time: 535 us -> 199 us (0.37)
  the two profiles are of different devices: /device:TPU:0 before, /device:TPU:15 now
where the time goes in v2:
time: 199 us
  waiting for transfers between devices  72 us (36%)
  Pallas kernels  65.4 us (33%)
  blocking collectives  36.5 us (18%)
  starting transfers between devices  17.1 us (9%)
  local copies, waits for them, and re-layouts  7.14 us (4%)
    all_to_all x3, waiting for transfers between devices, turn(): lax.all_to_all(x, ('freq', 'tm'), 0, 0, tiled=True).reshape(-1, LANES)  72 us
    all_to_all x1, blocking collectives, turn(): lax.all_to_all(x, ('freq', 'tm'), 0, 0, tiled=True).reshape(-1, LANES)  36.5 us
    pallas_call x1, Pallas kernels, local_tree(): pl.pallas_call(functools.partial(local_tree_kernel, levels, blocks, lead_...  35 us
    pallas_call x2, Pallas kernels, filter_rows(): pl.pallas_call(functools.partial(filter_kernel, per_step, blocks, filters...  18.5 us
    all_to_all x3, starting transfers between devices, turn(): lax.all_to_all(x, ('freq', 'tm'), 0, 0, tiled=True).reshape(-1, LANES)  14.5 us
    pallas_call x2, Pallas kernels, cross_tree(): pl.pallas_call(functools.partial(cross_kernel, bits, rows, own, group * r...  11.9 us
    unnamed x13, local copies, waits for them, and re-layouts  4.58 us
  transfers between devices with their start and end apart: 4, of which 3 were waited for; matrix products, arithmetic and copies ran while one was open for 1% of the time, Pallas kernels for 11%

profile of v2, /device:TPU:15, one launch (start us, length us, event | category | flops | bytes accessed | tf_op | source)
XLA Modules:
  0.0 198.8 jit_solution(701818393618015843)
XLA Ops:
  0.0 1.0 slice.10
  1.0 2.6 %collective-permute-start = (f32[256,256]{1,0:T(8,128)S(1)}, f32[256,256]{1,0:T(8,128)S(1)}, u32[]{:S(2)}, u32[]{:S(2)}) collective-permute-start(f32[256,256]{1,0:T(8,128)S(1)} %slice.10), channel_id=1, source_target_pairs={{1,0},{3,2},{5,4},{7,6},{9,8},{11,10},{13,12},{15,14},{17,16},{19,... | collective-permute-start | bytes 786440 | tf_op jit(solution)/shard_map/ppermute | solution.py:254
  3.6 0.8 slice.11
  4.4 0.6 copy.6
  5.0 0.0 collective-permute-done.lead
  5.0 0.7 copy-done.3
  5.7 35.0 %shard_map.37 = (f32[2560,128]{1,0:T(8,128)}, f32[2560,128]{1,0:T(8,128)}) custom-call(f32[256,2560]{1,0:T(8,128)} %spectra.1, f32[256,256]{1,0:T(8,128)} %copy-done.3, s32[2048]{0:T(1024)} %bitcast.25), custom_call_target="tpu_custom_call" | custom-call | tf_op jit(solution)/shard_map/pallas_call | solution.py:106
  40.7 36.5 %all_to_all.20 = f32[16,160,128]{2,1,0:T(8,128)} all-to-all(f32[16,160,128]{2,1,0:T(8,128)} %bitcast.22), channel_id=1, replica_groups=mesh['beam'=2,'freq'=8,'tm'=2] {'freq','tm'}, dimensions={0} | all-to-all | bytes 2621440 | tf_op jit(solution)/shard_map/all_to_all | solution.py:263
  77.2 5.1 %all-to-all-start = ((f32[16,160,128]{2,1,0:T(8,128)}), f32[16,160,128]{2,1,0:T(8,128)S(1)}, u32[]{:S(2)}, u32[]{:S(2)}) async-start(f32[16,160,128]{2,1,0:T(8,128)} %bitcast), calls=%async_computation | async-start | bytes 2621440 | tf_op jit(solution)/shard_map/all_to_all | solution.py:263
  82.3 0.1 constant_dynamic-slice_fusion
  82.4 0.7 reshape.37.shifts
  83.1 5.9 %shard_map.39 = f32[2688,128]{1,0:T(8,128)} custom-call(s32[384]{0:T(512)} %reshape.37.shifts, f32[2560,128]{1,0:T(8,128)} %bitcast.21), custom_call_target="tpu_custom_call" | custom-call | bytes 6881280 | tf_op jit(solution)/shard_map/pallas_call | solution.py:168
  89.0 23.9 %all-to-all-done = f32[16,160,128]{2,1,0:T(8,128)S(1)} async-done(((f32[16,160,128]{2,1,0:T(8,128)}), f32[16,160,128]{2,1,0:T(8,128)S(1)}, u32[]{:S(2)}, u32[]{:S(2)}) %all-to-all-start) | async-done | bytes 1310752 | tf_op jit(solution)/shard_map/all_to_all | solution.py:263
  112.9 1.1 copy-done.2
  113.9 4.7 %all-to-all-start.3 = ((f32[16,168,128]{2,1,0:T(8,128)}), f32[16,168,128]{2,1,0:T(8,128)S(1)}, u32[]{:S(2)}, u32[]{:S(2)}) async-start(f32[16,168,128]{2,1,0:T(8,128)} %bitcast.18), calls=%async_computation.3 | async-start | bytes 2752512 | tf_op jit(solution)/shard_map/all_to_all | solution.py:263
  118.7 6.0 %shard_map.38 = f32[2688,128]{1,0:T(8,128)} custom-call(s32[384]{0:T(512)} %reshape.37.shifts, f32[2560,128]{1,0:T(8,128)} %bitcast.20), custom_call_target="tpu_custom_call" | custom-call | bytes 6881280 | tf_op jit(solution)/shard_map/pallas_call | solution.py:168
  124.6 26.0 %all-to-all-done.3 = f32[16,168,128]{2,1,0:T(8,128)S(1)} async-done(((f32[16,168,128]{2,1,0:T(8,128)}), f32[16,168,128]{2,1,0:T(8,128)S(1)}, u32[]{:S(2)}, u32[]{:S(2)}) %all-to-all-start.3) | async-done | bytes 1376288 | tf_op jit(solution)/shard_map/all_to_all | solution.py:263
  150.6 1.1 copy-done.1
  151.7 4.7 %all-to-all-start.1 = ((f32[16,168,128]{2,1,0:T(8,128)}), f32[16,168,128]{2,1,0:T(8,128)S(1)}, u32[]{:S(2)}, u32[]{:S(2)}) async-start(f32[16,168,128]{2,1,0:T(8,128)} %bitcast.17), calls=%async_computation.1 | async-start | bytes 2752512 | tf_op jit(solution)/shard_map/all_to_all | solution.py:263
  156.5 0.5 multiply_rsqrt_fusion.scaling
  157.0 9.3 %shard_map.40.refs_0_ = f32[8,16,16,2560]{3,2,1,0:T(8,128)} custom-call(s32[8]{0:T(128)} %widths.3, f32[8]{0:T(128)} %multiply_rsqrt_fusion.scaling, f32[2688,128]{1,0:T(8,128)} %bitcast.19), custom_call_target="tpu_custom_call" | custom-call | flops 2684354560 | bytes 10485760 | tf_op jit(solution)/shard_map/pallas_call | solution.py:227
  166.3 22.2 %all-to-all-done.1 = f32[16,168,128]{2,1,0:T(8,128)S(1)} async-done(((f32[16,168,128]{2,1,0:T(8,128)}), f32[16,168,128]{2,1,0:T(8,128)S(1)}, u32[]{:S(2)}, u32[]{:S(2)}) %all-to-all-start.1) | async-done | bytes 1376288 | tf_op jit(solution)/shard_map/all_to_all | solution.py:263
  188.4 1.1 copy-done
  189.5 9.3 %shard_map.41 = f32[8,16,16,2560]{3,2,1,0:T(8,128)} custom-call(s32[8]{0:T(128)} %widths.3, f32[8]{0:T(128)} %multiply_rsqrt_fusion.scaling, f32[2688,128]{1,0:T(8,128)} %bitcast.16, f32[8,16,16,2560]{3,2,1,0:T(8,128)} %shard_map.40.refs_0_), custom_call_target="tpu_custom_call", output_to_operand_aliasing={{}: (3, {})} | custom-call | flops 2684354560 | bytes 10485760 | tf_op jit(solution)/shard_map/pallas_call | solution.py:227
  (10 shorter events, 0.0 us)
Async XLA Ops:
  1.0 4.1 %collective-permute-start = (f32[256,256]{1,0:T(8,128)S(1)}, f32[256,256]{1,0:T(8,128)S(1)}, u32[]{:S(2)}, u32[]{:S(2)}) collective-permute-start(f32[256,256]{1,0:T(8,128)S(1)} %slice.10), channel_id=1, source_target_pairs={{1,0},{3,2},{5,4},{7,6},{9,8},{11,10},{13,12},{15,14},{17,16},{19,... | collective-permute-start | bytes 786440 | tf_op jit(solution)/shard_map/ppermute | solution.py:254
  5.0 0.7 copy-start.3
  77.2 5.1 %slice-start = ((s32[11,2048]{1,0:T(8,128)}), s32[3,2048]{1,0:T(4,128)S(1)}, s32[]{:S(2)}) async-start(s32[11,2048]{1,0:T(8,128)} %param.4), calls=%async_computation.4 | async-start | bytes 65536 | tf_op jit(solution)/shard_map/slice | solution.py:257
  77.2 35.6 %all-to-all-start = ((f32[16,160,128]{2,1,0:T(8,128)}), f32[16,160,128]{2,1,0:T(8,128)S(1)}, u32[]{:S(2)}, u32[]{:S(2)}) async-start(f32[16,160,128]{2,1,0:T(8,128)} %bitcast), calls=%async_computation | async-start | bytes 2621440 | tf_op jit(solution)/shard_map/all_to_all | solution.py:263
  112.9 1.1 copy-start.2
  113.9 36.7 %all-to-all-start.3 = ((f32[16,168,128]{2,1,0:T(8,128)}), f32[16,168,128]{2,1,0:T(8,128)S(1)}, u32[]{:S(2)}, u32[]{:S(2)}) async-start(f32[16,168,128]{2,1,0:T(8,128)} %bitcast.18), calls=%async_computation.3 | async-start | bytes 2752512 | tf_op jit(solution)/shard_map/all_to_all | solution.py:263
  150.6 1.1 copy-start.1
  150.6 5.8 %copy-start.4 = (s32[8]{0:T(128)S(1)}, s32[8]{0:T(128)}, u32[]{:S(2)}) copy-start(s32[8]{0:T(128)} %widths.3) | copy-start | bytes 100
  151.7 36.7 %all-to-all-start.1 = ((f32[16,168,128]{2,1,0:T(8,128)}), f32[16,168,128]{2,1,0:T(8,128)S(1)}, u32[]{:S(2)}, u32[]{:S(2)}) async-start(f32[16,168,128]{2,1,0:T(8,128)} %bitcast.17), calls=%async_computation.1 | async-start | bytes 2752512 | tf_op jit(solution)/shard_map/all_to_all | solution.py:263
  188.4 1.1 copy-start

commit v3 on v2

--- a/solution.py
+++ b/solution.py
@@ -24,11 +24,11 @@
 
 def shifted(src, start, width, shift, reach, lane):
     if reach >= LANES:
-        start = start + shift // LANES
-        shift = shift % LANES
+        start = start + lax.shift_right_logical(shift, LANES.bit_length() - 1)
+        shift = shift & (LANES - 1)
     low = src[pl.ds(start, width), :]
     high = src[pl.ds(start + 1, width), :]
-    return pltpu.roll(jnp.where(lane < shift, high, low), (LANES - shift) % LANES, 1)
+    return pltpu.roll(jnp.where(lane < shift, high, low), LANES - shift, 1)
 
 
 def local_tree_kernel(levels, blocks, lead_blocks, own, pitch, spectra, lead, shifts, *refs):
@@ -36,6 +36,7 @@
     rows = spectra.shape[0]
     groups = len(outs)
     per = own // groups
+    per_bits, own_bits = per.bit_length() - 1, own.bit_length() - 1
     lane = lax.broadcasted_iota(jnp.int32, (pitch, LANES), 1)
     out_lane = lax.broadcasted_iota(jnp.int32, (blocks, LANES), 1)
 
@@ -54,12 +55,12 @@
     src, dst = buf_a, buf_b
     for level in range(levels - 1):
         half = 2**level
-        unroll = 4
+        unroll = min(8, rows // 2)
 
         def pairs(n, carry, src=src, dst=dst, half=half, level=level):
             for u in range(unroll):
                 p = n * unroll + u
-                row_a = (p // half) * (2 * half) + p % half
+                row_a = ((p >> level) << (level + 1)) + (p & (half - 1))
                 at_a = pl.multiple_of(row_a * pitch, SUB)
                 at_b = pl.multiple_of((row_a + half) * pitch, SUB)
                 a = src[pl.ds(at_a, pitch), :]
@@ -74,19 +75,19 @@
     level = levels - 1
     half = 2**level
     for group, out in enumerate(outs):
-        unroll = 4
+        unroll = 8 if rows // 2 // groups % 8 == 0 else 1
 
         def last_pairs(n, carry, src=src, out=out, group=group):
             for u in range(unroll):
                 m = n * unroll + u
-                row_a = (m // per) * own + group * per + m % per
+                row_a = (m >> per_bits) * own + group * per + (m & (per - 1))
                 at_a = pl.multiple_of(row_a * pitch, SUB)
                 at_b = pl.multiple_of((row_a + half) * pitch, SUB)
                 a = src[pl.ds(at_a, blocks), :]
                 for e in range(2):
                     row = row_a + e * half
                     shift = shifts[level * rows + row]
-                    at = ((row // own) * per + m % per) * blocks
+                    at = ((row >> own_bits) * per + (m & (per - 1))) * blocks
                     out[pl.ds(at, blocks), :] = a + shifted(src, at_b, blocks, shift, half, out_lane)
             return carry
 

time: 199 us -> 184 us (0.925)
  Pallas kernels: 65.4 us -> 48.8 us
    pallas_call x1, Pallas kernels: 35 us -> 19.4 us  [local_tree(): pl.pallas_call(functools.partial(local_tree_kernel, levels, blocks, lead_...]
where the time goes in v3:
time: 184 us; the launch traced here: 183 us
  waiting for transfers between devices  73.1 us (40%)
  Pallas kernels  48.8 us (27%)
  blocking collectives  36.5 us (20%)
  starting transfers between devices  17.1 us (9%)
  local copies, waits for them, and re-layouts  7.14 us (4%)
    all_to_all x3, waiting for transfers between devices, turn(): lax.all_to_all(x, ('freq', 'tm'), 0, 0, tiled=True).reshape(-1, LANES)  73.1 us
    all_to_all x1, blocking collectives, turn(): lax.all_to_all(x, ('freq', 'tm'), 0, 0, tiled=True).reshape(-1, LANES)  36.5 us
    pallas_call x1, Pallas kernels, local_tree(): pl.pallas_call(functools.partial(local_tree_kernel, levels, blocks, lead_...  19.4 us
    pallas_call x2, Pallas kernels, filter_rows(): pl.pallas_call(functools.partial(filter_kernel, per_step, blocks, filters...  18.5 us
    all_to_all x3, starting transfers between devices, turn(): lax.all_to_all(x, ('freq', 'tm'), 0, 0, tiled=True).reshape(-1, LANES)  14.5 us
    pallas_call x2, Pallas kernels, cross_tree(): pl.pallas_call(functools.partial(cross_kernel, bits, rows, own, group * r...  10.8 us
    unnamed x13, local copies, waits for them, and re-layouts  4.58 us
  transfers between devices with their start and end apart: 4, of which 3 were waited for; matrix products, arithmetic and copies ran while one was open for 1% of the time, Pallas kernels for 11%

profile of v3, /device:TPU:15, one launch (start us, length us, event | category | flops | bytes accessed | tf_op | source)
XLA Modules:
  0.0 183.2 jit_solution(5203862974068844881)
XLA Ops:
  0.0 1.0 slice.10
  1.0 2.6 %collective-permute-start = (f32[256,256]{1,0:T(8,128)S(1)}, f32[256,256]{1,0:T(8,128)S(1)}, u32[]{:S(2)}, u32[]{:S(2)}) collective-permute-start(f32[256,256]{1,0:T(8,128)S(1)} %slice.10), channel_id=1, source_target_pairs={{1,0},{3,2},{5,4},{7,6},{9,8},{11,10},{13,12},{15,14},{17,16},{19,... | collective-permute-start | bytes 786440 | tf_op jit(solution)/shard_map/ppermute | solution.py:255
  3.6 0.8 slice.11
  4.4 0.6 copy.6
  5.0 0.0 collective-permute-done.lead
  5.0 0.7 copy-done.3
  5.7 19.4 %shard_map.37 = (f32[2560,128]{1,0:T(8,128)}, f32[2560,128]{1,0:T(8,128)}) custom-call(f32[256,2560]{1,0:T(8,128)} %spectra.1, f32[256,256]{1,0:T(8,128)} %copy-done.3, s32[2048]{0:T(1024)} %bitcast.25), custom_call_target="tpu_custom_call" | custom-call | tf_op jit(solution)/shard_map/pallas_call | solution.py:107
  25.2 36.5 %all_to_all.20 = f32[16,160,128]{2,1,0:T(8,128)} all-to-all(f32[16,160,128]{2,1,0:T(8,128)} %bitcast.22), channel_id=1, replica_groups=mesh['beam'=2,'freq'=8,'tm'=2] {'freq','tm'}, dimensions={0} | all-to-all | bytes 2621440 | tf_op jit(solution)/shard_map/all_to_all | solution.py:264
  61.7 5.1 %all-to-all-start = ((f32[16,160,128]{2,1,0:T(8,128)}), f32[16,160,128]{2,1,0:T(8,128)S(1)}, u32[]{:S(2)}, u32[]{:S(2)}) async-start(f32[16,160,128]{2,1,0:T(8,128)} %bitcast), calls=%async_computation | async-start | bytes 2621440 | tf_op jit(solution)/shard_map/all_to_all | solution.py:264
  66.8 0.1 constant_dynamic-slice_fusion
  66.8 0.7 reshape.37.shifts
  67.5 5.4 %shard_map.39 = f32[2688,128]{1,0:T(8,128)} custom-call(s32[384]{0:T(512)} %reshape.37.shifts, f32[2560,128]{1,0:T(8,128)} %bitcast.21), custom_call_target="tpu_custom_call" | custom-call | bytes 6881280 | tf_op jit(solution)/shard_map/pallas_call | solution.py:169
  72.9 24.4 %all-to-all-done = f32[16,160,128]{2,1,0:T(8,128)S(1)} async-done(((f32[16,160,128]{2,1,0:T(8,128)}), f32[16,160,128]{2,1,0:T(8,128)S(1)}, u32[]{:S(2)}, u32[]{:S(2)}) %all-to-all-start) | async-done | bytes 1310752 | tf_op jit(solution)/shard_map/all_to_all | solution.py:264
  97.3 1.1 copy-done.2
  98.4 4.7 %all-to-all-start.3 = ((f32[16,168,128]{2,1,0:T(8,128)}), f32[16,168,128]{2,1,0:T(8,128)S(1)}, u32[]{:S(2)}, u32[]{:S(2)}) async-start(f32[16,168,128]{2,1,0:T(8,128)} %bitcast.18), calls=%async_computation.3 | async-start | bytes 2752512 | tf_op jit(solution)/shard_map/all_to_all | solution.py:264
  103.1 5.4 %shard_map.38 = f32[2688,128]{1,0:T(8,128)} custom-call(s32[384]{0:T(512)} %reshape.37.shifts, f32[2560,128]{1,0:T(8,128)} %bitcast.20), custom_call_target="tpu_custom_call" | custom-call | bytes 6881280 | tf_op jit(solution)/shard_map/pallas_call | solution.py:169
  108.6 26.5 %all-to-all-done.3 = f32[16,168,128]{2,1,0:T(8,128)S(1)} async-done(((f32[16,168,128]{2,1,0:T(8,128)}), f32[16,168,128]{2,1,0:T(8,128)S(1)}, u32[]{:S(2)}, u32[]{:S(2)}) %all-to-all-start.3) | async-done | bytes 1376288 | tf_op jit(solution)/shard_map/all_to_all | solution.py:264
  135.1 1.1 copy-done.1
  136.2 4.7 %all-to-all-start.1 = ((f32[16,168,128]{2,1,0:T(8,128)}), f32[16,168,128]{2,1,0:T(8,128)S(1)}, u32[]{:S(2)}, u32[]{:S(2)}) async-start(f32[16,168,128]{2,1,0:T(8,128)} %bitcast.17), calls=%async_computation.1 | async-start | bytes 2752512 | tf_op jit(solution)/shard_map/all_to_all | solution.py:264
  140.9 0.5 multiply_rsqrt_fusion.scaling
  141.4 9.3 %shard_map.40.refs_0_ = f32[8,16,16,2560]{3,2,1,0:T(8,128)} custom-call(s32[8]{0:T(128)} %widths.3, f32[8]{0:T(128)} %multiply_rsqrt_fusion.scaling, f32[2688,128]{1,0:T(8,128)} %bitcast.19), custom_call_target="tpu_custom_call" | custom-call | flops 2684354560 | bytes 10485760 | tf_op jit(solution)/shard_map/pallas_call | solution.py:228
  150.7 22.2 %all-to-all-done.1 = f32[16,168,128]{2,1,0:T(8,128)S(1)} async-done(((f32[16,168,128]{2,1,0:T(8,128)}), f32[16,168,128]{2,1,0:T(8,128)S(1)}, u32[]{:S(2)}, u32[]{:S(2)}) %all-to-all-start.1) | async-done | bytes 1376288 | tf_op jit(solution)/shard_map/all_to_all | solution.py:264
  172.9 1.1 copy-done
  174.0 9.3 %shard_map.41 = f32[8,16,16,2560]{3,2,1,0:T(8,128)} custom-call(s32[8]{0:T(128)} %widths.3, f32[8]{0:T(128)} %multiply_rsqrt_fusion.scaling, f32[2688,128]{1,0:T(8,128)} %bitcast.16, f32[8,16,16,2560]{3,2,1,0:T(8,128)} %shard_map.40.refs_0_), custom_call_target="tpu_custom_call", output_to_operand_aliasing={{}: (3, {})} | custom-call | flops 2684354560 | bytes 10485760 | tf_op jit(solution)/shard_map/pallas_call | solution.py:228
  (10 shorter events, 0.0 us)
Async XLA Ops:
  1.0 4.1 %collective-permute-start = (f32[256,256]{1,0:T(8,128)S(1)}, f32[256,256]{1,0:T(8,128)S(1)}, u32[]{:S(2)}, u32[]{:S(2)}) collective-permute-start(f32[256,256]{1,0:T(8,128)S(1)} %slice.10), channel_id=1, source_target_pairs={{1,0},{3,2},{5,4},{7,6},{9,8},{11,10},{13,12},{15,14},{17,16},{19,... | collective-permute-start | bytes 786440 | tf_op jit(solution)/shard_map/ppermute | solution.py:255
  5.0 0.7 copy-start.3
  61.7 5.1 %slice-start = ((s32[11,2048]{1,0:T(8,128)}), s32[3,2048]{1,0:T(4,128)S(1)}, s32[]{:S(2)}) async-start(s32[11,2048]{1,0:T(8,128)} %param.4), calls=%async_computation.4 | async-start | bytes 65536 | tf_op jit(solution)/shard_map/slice | solution.py:258
  61.7 35.6 %all-to-all-start = ((f32[16,160,128]{2,1,0:T(8,128)}), f32[16,160,128]{2,1,0:T(8,128)S(1)}, u32[]{:S(2)}, u32[]{:S(2)}) async-start(f32[16,160,128]{2,1,0:T(8,128)} %bitcast), calls=%async_computation | async-start | bytes 2621440 | tf_op jit(solution)/shard_map/all_to_all | solution.py:264
  97.3 1.1 copy-start.2
  98.4 36.7 %all-to-all-start.3 = ((f32[16,168,128]{2,1,0:T(8,128)}), f32[16,168,128]{2,1,0:T(8,128)S(1)}, u32[]{:S(2)}, u32[]{:S(2)}) async-start(f32[16,168,128]{2,1,0:T(8,128)} %bitcast.18), calls=%async_computation.3 | async-start | bytes 2752512 | tf_op jit(solution)/shard_map/all_to_all | solution.py:264
  135.1 1.1 copy-start.1
  135.1 5.8 %copy-start.4 = (s32[8]{0:T(128)S(1)}, s32[8]{0:T(128)}, u32[]{:S(2)}) copy-start(s32[8]{0:T(128)} %widths.3) | copy-start | bytes 100
  136.2 36.7 %all-to-all-start.1 = ((f32[16,168,128]{2,1,0:T(8,128)}), f32[16,168,128]{2,1,0:T(8,128)S(1)}, u32[]{:S(2)}, u32[]{:S(2)}) async-start(f32[16,168,128]{2,1,0:T(8,128)} %bitcast.17), calls=%async_computation.1 | async-start | bytes 2752512 | tf_op jit(solution)/shard_map/all_to_all | solution.py:264
  172.9 1.1 copy-start

commit v4 on v3

--- a/solution.py
+++ b/solution.py
@@ -113,69 +113,134 @@
     )(spectra, lead, shifts)
 
 
-def cross_kernel(bits, rows, own, first, blocks, halves, pitch, first_level, shifts, arrived, out, buf_a, buf_b):
+def turn_kernel(bits, rows, blocks, halves, pitch, first_level, groups, shifts, *refs):
+    xs, outs = refs[:groups], refs[groups : 2 * groups]
+    arrived, ready = refs[2 * groups : 3 * groups], refs[3 * groups : 4 * groups]
+    buf_a, buf_b, sems, own_sems = refs[4 * groups :]
+    own = rows * groups
     total = blocks * halves
     bands = 2**bits
+    parts = bands * halves
     out_blocks = blocks + 1
+    me = lax.axis_index("freq") * halves + lax.axis_index("tm")
+    beam = lax.axis_index("beam")
+
+    def device(k):
+        other = (me + k) % parts
+        return other, (beam, other // halves, other % halves)
+
+    barrier = pltpu.get_barrier_semaphore()
+    for k in range(1, parts):
+        pl.semaphore_signal(
+            barrier, inc=1, device_id=device(k)[1], device_id_type=pl.DeviceIdType.MESH
+        )
+    pl.semaphore_wait(barrier, parts - 1)
+
+    def send(src, dst, turn):
+        copies = []
+        for k in range(1, parts):
+            other, where = device(k)
+            c = pltpu.make_async_remote_copy(
+                src_ref=src.at[other],
+                dst_ref=dst.at[me],
+                send_sem=sems.at[0, turn, k],
+                recv_sem=sems.at[1, turn, k],
+                device_id=where,
+                device_id_type=pl.DeviceIdType.MESH,
+            )
+            c.start()
+            copies.append(c)
+        c = pltpu.make_async_copy(src.at[me], dst.at[me], own_sems.at[turn])
+        c.start()
+        copies.append(c)
+        return copies
+
+    def wait(copies):
+        for c in copies:
+            c.wait()
+
+    first = [send(xs[g], arrived[g], g) for g in range(groups)]
+
     lane = lax.broadcasted_iota(jnp.int32, (total, LANES), 1)
     out_lane = lax.broadcasted_iota(jnp.int32, (out_blocks, LANES), 1)
     zero = jnp.zeros((pitch - total, LANES), jnp.float32)
 
-    def gather(i, carry):
-        for s in range(bands):
-            at = (s * rows + i) * pitch
-            for c in range(halves):
-                piece = arrived[pl.ds(((s * halves + c) * rows + i) * blocks, blocks), :]
-                buf_a[pl.ds(at + c * blocks, blocks), :] = piece
-            for buf in (buf_a, buf_b):
-                buf[pl.ds(at + total, pitch - total), :] = zero
+    def clear(r, carry):
+        for buf in (buf_a, buf_b):
+            buf[pl.ds(r * pitch + total, pitch - total), :] = zero
         return carry
 
-    lax.fori_loop(0, rows, gather, 0)
-
-    src, dst = buf_a, buf_b
-    for level in range(bits):
-        step = 2**level
-        reach = 2 ** (first_level + level)
-
-        def one_row(i, carry, src=src, dst=dst, step=step, level=level, reach=reach):
-            for j in range(bands):
-                base = (j // (2 * step)) * (2 * step) + j % step
-                shift = shifts[(level * bands + j) * own + first + i]
-                at_a = pl.multiple_of((base * rows + i) * pitch, SUB)
-                at_b = pl.multiple_of(((base + step) * rows + i) * pitch, SUB)
-                if level < bits - 1:
-                    a = src[pl.ds(at_a, total), :]
-                    at = pl.multiple_of((j * rows + i) * pitch, SUB)
-                    dst[pl.ds(at, total), :] = a + shifted(src, at_b, total, shift, reach, lane)
-                    continue
+    lax.fori_loop(0, bands * rows, clear, 0)
+    for buf in (buf_a, buf_b):
+        buf[pl.ds(bands * rows * pitch, SUB), :] = jnp.zeros((SUB, LANES), jnp.float32)
+
+    back = []
+    for g in range(groups):
+        wait(first[g])
+
+        def gather(i, carry, g=g):
+            for s in range(bands):
+                at = (s * rows + i) * pitch
                 for c in range(halves):
-                    a = src[pl.ds(at_a + c * blocks, out_blocks), :]
-                    moved = shifted(src, at_b + c * blocks, out_blocks, shift, reach, out_lane)
-                    out[pl.ds(((j * halves + c) * rows + i) * out_blocks, out_blocks), :] = a + moved
+                    piece = arrived[g][s * halves + c, pl.ds(i * blocks, blocks), :]
+                    buf_a[pl.ds(at + c * blocks, blocks), :] = piece
             return carry
 
-        lax.fori_loop(0, rows, one_row, 0)
-        src, dst = dst, src
-
-
-def cross_tree(arrived, shifts, bits, own, group, groups, blocks, halves, first_level):
+        lax.fori_loop(0, rows, gather, 0)
+
+        src, dst = buf_a, buf_b
+        for level in range(bits):
+            step = 2**level
+            reach = 2 ** (first_level + level)
+
+            def one_row(i, carry, src=src, dst=dst, step=step, level=level, reach=reach, g=g):
+                for j in range(bands):
+                    base = (j // (2 * step)) * (2 * step) + j % step
+                    shift = shifts[(level * bands + j) * own + g * rows + i]
+                    at_a = pl.multiple_of((base * rows + i) * pitch, SUB)
+                    at_b = pl.multiple_of(((base + step) * rows + i) * pitch, SUB)
+                    if level < bits - 1:
+                        a = src[pl.ds(at_a, total), :]
+                        at = pl.multiple_of((j * rows + i) * pitch, SUB)
+                        dst[pl.ds(at, total), :] = a + shifted(src, at_b, total, shift, reach, lane)
+                        continue
+                    for c in range(halves):
+                        a = src[pl.ds(at_a + c * blocks, out_blocks), :]
+                        moved = shifted(src, at_b + c * blocks, out_blocks, shift, reach, out_lane)
+                        ready[g][j * halves + c, pl.ds(i * out_blocks, out_blocks), :] = a + moved
+                return carry
+
+            lax.fori_loop(0, rows, one_row, 0)
+            src, dst = dst, src
+        back.append(send(ready[g], outs[g], groups + g))
+    for copies in back:
+        wait(copies)
+
+
+def turn_and_cross(sections, shifts, bits, own, blocks, halves, first_level):
+    groups = len(sections)
     bands = 2**bits
+    parts = bands * halves
     reach = 2 ** (first_level + bits - 1)
     pitch = round_up(blocks * halves + cdiv(reach, LANES) + 2, SUB)
     rows = own // groups
     buf = pltpu.VMEM((bands * rows * pitch + SUB, LANES), jnp.float32)
-    out_rows = bands * halves * (blocks + 1) * rows
+    here = pl.BlockSpec(memory_space=pl.ANY)
+    out_shape = jax.ShapeDtypeStruct((parts, rows * (blocks + 1), LANES), jnp.float32)
     return pl.pallas_call(
-        functools.partial(
-            cross_kernel, bits, rows, own, group * rows, blocks, halves, pitch, first_level
-        ),
-        out_shape=jax.ShapeDtypeStruct((out_rows, LANES), jnp.float32),
-        in_specs=[pl.BlockSpec(memory_space=SMEM), pl.BlockSpec(memory_space=VMEM)],
-        out_specs=pl.BlockSpec(memory_space=VMEM),
-        scratch_shapes=[buf, buf],
-        cost_estimate=pl.CostEstimate(flops=0, bytes_accessed=20 * out_rows * LANES, transcendentals=0),
-    )(shifts, arrived)
+        functools.partial(turn_kernel, bits, rows, blocks, halves, pitch, first_level, groups),
+        out_shape=[out_shape] * groups,
+        in_specs=[pl.BlockSpec(memory_space=SMEM)] + [here] * groups,
+        out_specs=[here] * groups,
+        scratch_shapes=[pltpu.VMEM((parts, rows * blocks, LANES), jnp.float32)] * groups
+        + [pltpu.VMEM((parts, rows * (blocks + 1), LANES), jnp.float32)] * groups
+        + [buf, buf]
+        + [
+            pltpu.SemaphoreType.DMA((2, 2 * groups, parts)),
+            pltpu.SemaphoreType.DMA((2 * groups,)),
+        ],
+        compiler_params=pltpu.CompilerParams(collective_id=0, has_side_effects=True),
+    )(shifts, *sections)
 
 
 def filter_kernel(per_step, blocks, filters, widths, scaling, x, *refs):
@@ -259,17 +324,12 @@
     shifts = shifts.reshape(-1)
     scaling = 1.0 / jnp.sqrt(widths.astype(jnp.float32) * all_rows)
 
-    def turn(x):
-        x = x.reshape(parts, -1, LANES)
-        return lax.all_to_all(x, ("freq", "tm"), 0, 0, tiled=True).reshape(-1, LANES)
-
-    sections = [turn(x) for x in local_tree(spectra, lead, own_shifts, parts, groups)]
-    rows_done = [
-        turn(cross_tree(x, shifts, bits, own, g, groups, blocks, halves, levels))
-        for g, x in enumerate(sections)
-    ]
+    sections = local_tree(spectra, lead, own_shifts, parts, groups)
+    sections = [x.reshape(parts, -1, LANES) for x in sections]
+    rows_done = turn_and_cross(sections, shifts, bits, own, blocks, halves, levels)
     filtered = None
     for g, x in enumerate(rows_done):
+        x = x.reshape(-1, LANES)
         filtered = filter_rows(x, filtered, widths, scaling, parts, own, g, groups, blocks)
     return filtered.reshape(widths.shape[0], rows, span)
 

time: 184 us -> 170 us (0.924)
  Pallas kernels: 48.8 us -> 161 us
  waiting for transfers between devices: 73.1 us -> 0.01 us
  blocking collectives: 36.5 us -> 0 us
  starting transfers between devices: 17.1 us -> 2.6 us
  local copies, waits for them, and re-layouts: 7.14 us -> 4.7 us
    pallas_call x2 -> x1, Pallas kernels: 10.8 us -> 123 us  [turn_and_cross(): pl.pallas_call(functools.partial(turn_kernel, bits, rows, blocks, halves,...]
    all_to_all x3 -> x0, waiting for transfers between devices: 73.1 us -> none  [turn(): lax.all_to_all(x, ('freq', 'tm'), 0, 0, tiled=True).reshape(-1, LANES)]
    all_to_all x1 -> x0, blocking collectives: 36.5 us -> none  [turn(): lax.all_to_all(x, ('freq', 'tm'), 0, 0, tiled=True).reshape(-1, LANES)]
    all_to_all x3 -> x0, starting transfers between devices: 14.5 us -> none  [turn(): lax.all_to_all(x, ('freq', 'tm'), 0, 0, tiled=True).reshape(-1, LANES)]
    unnamed x13 -> x5, local copies, waits for them, and re-layouts: 4.58 us -> 1.29 us
  transfers between devices with their start and end apart: 4 -> 1, of which waited for: 3 -> 0; matrix products, arithmetic and copies ran while one was open for 1% -> 3% of each run, Pallas kernels for 11% -> 0%
where the time goes in v4:
time: 170 us
  Pallas kernels  161 us (95%)
  local copies, waits for them, and re-layouts  4.7 us (3%)
  starting transfers between devices  2.6 us (2%)
    pallas_call x1, Pallas kernels, turn_and_cross(): pl.pallas_call(functools.partial(turn_kernel, bits, rows, blocks, halves,...  123 us
    pallas_call x1, Pallas kernels, local_tree(): pl.pallas_call(functools.partial(local_tree_kernel, levels, blocks, lead_...  19.4 us
    pallas_call x2, Pallas kernels, filter_rows(): pl.pallas_call(functools.partial(filter_kernel, per_step, blocks, filters...  18.6 us
  transfers between devices with their start and end apart: 1, of which 0 were waited for; matrix products, arithmetic and copies ran while one was open for 3% of the time, Pallas kernels for 0%

profile of v4, /device:TPU:15, one launch (start us, length us, event | category | flops | bytes accessed | tf_op | source)
XLA Modules:
  0.0 170.0 jit_solution(9186736631520016830)
XLA Ops:
  0.0 1.0 slice.10
  1.0 2.6 %collective-permute-start = (f32[256,256]{1,0:T(8,128)S(1)}, f32[256,256]{1,0:T(8,128)S(1)}, u32[]{:S(2)}, u32[]{:S(2)}) collective-permute-start(f32[256,256]{1,0:T(8,128)S(1)} %slice.10), channel_id=1, source_target_pairs={{1,0},{3,2},{5,4},{7,6},{9,8},{11,10},{13,12},{15,14},{17,16},{19,... | collective-permute-start | bytes 786440 | tf_op jit(solution)/shard_map/ppermute | solution.py:320
  3.6 0.8 slice.9
  4.4 0.8 slice.11
  5.3 0.1 constant_dynamic-slice_fusion
  5.4 0.7 reshape.25.shifts
  6.0 0.6 copy.6
  6.6 1.3 multiply_rsqrt_fusion.scaling
  7.9 0.0 collective-permute-done.lead
  7.9 0.0 copy-start
  7.9 0.7 copy-done
  8.6 19.4 %shard_map.37 = (f32[2560,128]{1,0:T(8,128)}, f32[2560,128]{1,0:T(8,128)}) custom-call(f32[256,2560]{1,0:T(8,128)} %spectra.1, f32[256,256]{1,0:T(8,128)} %copy-done, s32[2048]{0:T(1024)} %bitcast.18), custom_call_target="tpu_custom_call" | custom-call | tf_op jit(solution)/shard_map/pallas_call | solution.py:107
  28.0 123.4 %shard_map.38 = (f32[16,168,128]{2,1,0:T(8,128)}, f32[16,168,128]{2,1,0:T(8,128)}) custom-call(s32[384]{0:T(512)} %reshape.25.shifts, f32[16,160,128]{2,1,0:T(8,128)} %bitcast.14, f32[16,160,128]{2,1,0:T(8,128)} %bitcast.15), custom_call_target="tpu_custom_call" | custom-call | tf_op jit(solution)/shard_map/pallas_call | solution.py:230
  151.4 9.3 %shard_map.39.refs_0_ = f32[8,16,16,2560]{3,2,1,0:T(8,128)} custom-call(s32[8]{0:T(128)} %widths.3, f32[8]{0:T(128)} %multiply_rsqrt_fusion.scaling, f32[2688,128]{1,0:T(8,128)} %bitcast.13), custom_call_target="tpu_custom_call" | custom-call | flops 2684354560 | bytes 10485760 | tf_op jit(solution)/shard_map/pallas_call | solution.py:293
  160.7 9.3 %shard_map.40 = f32[8,16,16,2560]{3,2,1,0:T(8,128)} custom-call(s32[8]{0:T(128)} %widths.3, f32[8]{0:T(128)} %multiply_rsqrt_fusion.scaling, f32[2688,128]{1,0:T(8,128)} %bitcast.12, f32[8,16,16,2560]{3,2,1,0:T(8,128)} %shard_map.39.refs_0_), custom_call_target="tpu_custom_call", output_to_operand_aliasing={{}: (3, {})} | custom-call | flops 2684354560 | bytes 10485760 | tf_op jit(solution)/shard_map/pallas_call | solution.py:293
  (2 shorter events, 0.0 us)
Async XLA Ops:
  1.0 6.9 %collective-permute-start = (f32[256,256]{1,0:T(8,128)S(1)}, f32[256,256]{1,0:T(8,128)S(1)}, u32[]{:S(2)}, u32[]{:S(2)}) collective-permute-start(f32[256,256]{1,0:T(8,128)S(1)} %slice.10), channel_id=1, source_target_pairs={{1,0},{3,2},{5,4},{7,6},{9,8},{11,10},{13,12},{15,14},{17,16},{19,... | collective-permute-start | bytes 786440 | tf_op jit(solution)/shard_map/ppermute | solution.py:320
  7.9 0.7 copy-start

commit v5 on v4

--- a/solution.py
+++ b/solution.py
@@ -274,7 +274,7 @@
 
 def filter_rows(x, into, widths, scaling, parts, own, group, groups, blocks):
     filters = widths.shape[0]
-    per_step = 2 if blocks % 2 == 0 else 1
+    per_step = 4 if blocks % 4 == 0 else 1
     rows = own // groups
     if rows % SUB:
         view, block, where = (filters, 1, parts * own), (filters, 1, parts * own), (0, 0, 0)

time: 170 us -> 168 us (0.988)
  Pallas kernels: 161 us -> 159 us
    pallas_call x2, Pallas kernels: 18.6 us -> 15.9 us  [filter_rows(): pl.pallas_call(functools.partial(filter_kernel, per_step, blocks, filters...]
where the time goes in v5:
time: 168 us; the launch traced here: 167 us
  Pallas kernels  159 us (95%)
  local copies, waits for them, and re-layouts  4.7 us (3%)
  starting transfers between devices  2.6 us (2%)
    pallas_call x1, Pallas kernels, turn_and_cross(): pl.pallas_call(functools.partial(turn_kernel, bits, rows, blocks, halves,...  123 us
    pallas_call x1, Pallas kernels, local_tree(): pl.pallas_call(functools.partial(local_tree_kernel, levels, blocks, lead_...  19.4 us
    pallas_call x2, Pallas kernels, filter_rows(): pl.pallas_call(functools.partial(filter_kernel, per_step, blocks, filters...  15.9 us
  transfers between devices with their start and end apart: 1, of which 0 were waited for; matrix products, arithmetic and copies ran while one was open for 3% of the time, Pallas kernels for 0%

profile of v5, /device:TPU:15, one launch (start us, length us, event | category | flops | bytes accessed | tf_op | source)
XLA Modules:
  0.0 167.3 jit_solution(962272217966177691)
XLA Ops:
  0.0 1.0 slice.10
  1.0 2.6 %collective-permute-start = (f32[256,256]{1,0:T(8,128)S(1)}, f32[256,256]{1,0:T(8,128)S(1)}, u32[]{:S(2)}, u32[]{:S(2)}) collective-permute-start(f32[256,256]{1,0:T(8,128)S(1)} %slice.10), channel_id=1, source_target_pairs={{1,0},{3,2},{5,4},{7,6},{9,8},{11,10},{13,12},{15,14},{17,16},{19,... | collective-permute-start | bytes 786440 | tf_op jit(solution)/shard_map/ppermute | solution.py:320
  3.6 0.8 slice.9
  4.4 0.8 slice.11
  5.3 0.1 constant_dynamic-slice_fusion
  5.4 0.7 reshape.25.shifts
  6.0 0.6 copy.6
  6.6 1.3 multiply_rsqrt_fusion.scaling
  7.9 0.0 collective-permute-done.lead
  7.9 0.0 copy-start
  7.9 0.7 copy-done
  8.6 19.4 %shard_map.37 = (f32[2560,128]{1,0:T(8,128)}, f32[2560,128]{1,0:T(8,128)}) custom-call(f32[256,2560]{1,0:T(8,128)} %spectra.1, f32[256,256]{1,0:T(8,128)} %copy-done, s32[2048]{0:T(1024)} %bitcast.18), custom_call_target="tpu_custom_call" | custom-call | tf_op jit(solution)/shard_map/pallas_call | solution.py:107
  28.0 123.4 %shard_map.38 = (f32[16,168,128]{2,1,0:T(8,128)}, f32[16,168,128]{2,1,0:T(8,128)}) custom-call(s32[384]{0:T(512)} %reshape.25.shifts, f32[16,160,128]{2,1,0:T(8,128)} %bitcast.14, f32[16,160,128]{2,1,0:T(8,128)} %bitcast.15), custom_call_target="tpu_custom_call" | custom-call | tf_op jit(solution)/shard_map/pallas_call | solution.py:230
  151.4 8.0 %shard_map.39.refs_0_ = f32[8,16,16,2560]{3,2,1,0:T(8,128)} custom-call(s32[8]{0:T(128)} %widths.3, f32[8]{0:T(128)} %multiply_rsqrt_fusion.scaling, f32[2688,128]{1,0:T(8,128)} %bitcast.13), custom_call_target="tpu_custom_call" | custom-call | flops 2684354560 | bytes 10485760 | tf_op jit(solution)/shard_map/pallas_call | solution.py:293
  159.4 7.9 %shard_map.40 = f32[8,16,16,2560]{3,2,1,0:T(8,128)} custom-call(s32[8]{0:T(128)} %widths.3, f32[8]{0:T(128)} %multiply_rsqrt_fusion.scaling, f32[2688,128]{1,0:T(8,128)} %bitcast.12, f32[8,16,16,2560]{3,2,1,0:T(8,128)} %shard_map.39.refs_0_), custom_call_target="tpu_custom_call", output_to_operand_aliasing={{}: (3, {})} | custom-call | flops 2684354560 | bytes 10485760 | tf_op jit(solution)/shard_map/pallas_call | solution.py:293
  (2 shorter events, 0.0 us)
Async XLA Ops:
  1.0 6.9 %collective-permute-start = (f32[256,256]{1,0:T(8,128)S(1)}, f32[256,256]{1,0:T(8,128)S(1)}, u32[]{:S(2)}, u32[]{:S(2)}) collective-permute-start(f32[256,256]{1,0:T(8,128)S(1)} %slice.10), channel_id=1, source_target_pairs={{1,0},{3,2},{5,4},{7,6},{9,8},{11,10},{13,12},{15,14},{17,16},{19,... | collective-permute-start | bytes 786440 | tf_op jit(solution)/shard_map/ppermute | solution.py:320
  7.9 0.7 copy-start
